TPU v7x, 512 devices: a whole 4x4x16 slice. The times are simulated.
512 devices in a mesh: seq: 64 (over z, y), tp: 8 (over x, core).
Axes of the slice: x: 4, y: 4, z: 16, core: 2. Of those that a mesh axis runs over, the one named last changes fastest.
Arguments:
- hidden: bfloat16 [384, 2048], P(None, 'seq'), may hold values from -12 to 12
- ln1_gain: float32 [2048], P('seq'), may hold values from 0.1 to 1.9
- wq: bfloat16 [2048, 2048], P('seq', 'tp'), may hold values from -0.125 to 0.125
- wk: bfloat16 [2048, 1024], P('seq', 'tp'), may hold values from -0.125 to 0.125
- wv: bfloat16 [2048, 1024], P('seq', 'tp'), may hold values from -0.125 to 0.125
- wg: bfloat16 [2048, 2048], P('seq', 'tp'), may hold values from -0.125 to 0.125
- q_gain: float32 [128], replicated, may hold values from 1 to 30
- key_gain: float32 [128], replicated, may hold values from 0.5 to 1.5
- wo: bfloat16 [2048, 2048], P('tp', 'seq'), may hold values from -0.5 to 0.5
- ln2_gain: float32 [2048], P('seq'), may hold values from 0.1 to 1.9
- w_gate: bfloat16 [2048, 6144], P('seq', 'tp'), may hold values from -0.125 to 0.125
- w_up: bfloat16 [2048, 6144], P('seq', 'tp'), may hold values from -0.125 to 0.125
- w_down: bfloat16 [6144, 2048], P('tp', 'seq'), may hold values from -0.078125 to 0.078125
- last_gain: float32 [2048], P('seq'), may hold values from 0.1 to 1.9
- head_weight: bfloat16 [2048, 131072], P(None, ('seq', 'tp')), may hold values from -0.125 to 0.125
- inv_temp: float32 [8], replicated, may hold values from 0.5 to 64
- key_cache: bfloat16 [8, 16384, 1024], P(None, 'seq', 'tp'), may hold values from -40 to 40
- value_cache: bfloat16 [8, 16384, 1024], P(None, 'seq', 'tp'), may hold values from -6 to 6
- lengths: int32 [8], replicated, may hold values from 1 to 16336
- parents: int32 [8, 48], replicated, may hold values from 0 to 46, as said below
- accepted: int32 [8], replicated, may hold values from 0 to 47
Outputs:
- logprobs: float32 [384, 131072], P(None, ('seq', 'tp'))
- next_hidden: bfloat16 [384, 2048], P(None, 'seq')
- updated_key_cache: bfloat16 [8, 16384, 1024], P(None, 'seq', 'tp')
- updated_value_cache: bfloat16 [8, 16384, 1024], P(None, 'seq', 'tp')
Inputs may be any that keep to these rules, and one draw needn't show every extreme that they name: parents[r, 0] = 0; for i >= 1, i - 4 <= parents[r, i] < i.
All inputs are finite; a program needn't handle non-finite values.
Results may differ from a plain program's by a relative error of at most 0.012.
Values may be sent and summed in bfloat16 or wider, within the bound.
No kernel may reach another device: no remote copies, remote signals or barrier semaphores. Data moves between devices by JAX's collectives and lax.ppermute only.
A program may use at most 128 MiB of HBM per device.

v0:
```python
import jax
import jax.numpy as jnp
from jax import lax
from jax.sharding import PartitionSpec as P

EPSILON = 1e-06
ROPE_BASE = 1000000.0
NEGATIVE = -1e30


def ancestry(parents):
    node_count = parents.shape[-1]
    node_ids = jnp.arange(node_count, dtype=jnp.int32)
    reachable = (parents[..., :, None] == node_ids[None, :]).astype(jnp.float32)
    reachable = jnp.maximum(reachable, jnp.eye(node_count, dtype=jnp.float32))
    for turn in range((node_count - 1).bit_length()):
        reachable = jnp.minimum(
            jnp.einsum("rij,rjk->rik", reachable, reachable, precision=lax.Precision.HIGHEST), 1.0
        )
    return reachable


def head_norm(values, gain):
    meansq = jnp.mean(values * values, axis=-1, keepdims=True)
    return values * lax.rsqrt(meansq + EPSILON) * gain


def apply_rotary(values, places):
    half_dim = values.shape[-1] // 2
    spread = ROPE_BASE ** (-jnp.arange(half_dim, dtype=jnp.float32) / half_dim)
    angles = places.astype(jnp.float32)[:, None] * spread[None, :]
    cosine = jnp.cos(angles)[:, None, :]
    sine = jnp.sin(angles)[:, None, :]
    lower_part = values[..., :half_dim]
    upper_part = values[..., half_dim:]
    return jnp.concatenate(
        [lower_part * cosine - upper_part * sine, upper_part * cosine + lower_part * sine], axis=-1
    )


def cache_part(query_blocks, key_block, value_block, valid_slot):
    scores = jnp.einsum(
        "rikgd,rckd->rkgic", query_blocks, key_block, preferred_element_type=jnp.float32
    )
    valid_slot = valid_slot[:, None, None, None, :]
    row_peak = jnp.max(jnp.where(valid_slot, scores, NEGATIVE), axis=-1)
    weights = jnp.where(valid_slot, jnp.exp(scores - row_peak[..., None]), 0.0)
    row_mass = jnp.sum(weights, axis=-1)
    weighted = jnp.einsum(
        "rkgic,rckd->rkgid",
        weights.astype(jnp.bfloat16),
        value_block,
        preferred_element_type=jnp.float32,
    )
    return (row_peak, row_mass, weighted)


def on_device(
    hidden,
    ln1_gain,
    wq,
    wk,
    wv,
    wg,
    q_gain,
    key_gain,
    wo,
    ln2_gain,
    w_gate,
    w_up,
    w_down,
    last_gain,
    head_weight,
    inv_temp,
    key_cache,
    value_cache,
    lengths,
    parents,
    accepted,
):
    seq_count = lax.axis_size("seq")
    model_width = hidden.shape[1] * seq_count
    head_dim = q_gain.shape[0]
    query_heads = wq.shape[1] // head_dim
    kv_heads = wk.shape[1] // head_dim
    query_group_size = query_heads // kv_heads
    requests, tree_size = parents.shape
    token_count = hidden.shape[0]
    slot_count = key_cache.shape[1]
    slot_start = lax.axis_index("seq") * slot_count
    parent_links = ancestry(parents)
    tree_node_depth = jnp.sum((parent_links > 0.5).astype(jnp.int32), axis=-1) - 1
    token_position = (lengths[:, None] + tree_node_depth).reshape(-1)
    hidden_wide = hidden.astype(jnp.float32)
    squares = lax.psum(jnp.sum(hidden_wide * hidden_wide, axis=1), "seq")
    normed1 = (hidden_wide * lax.rsqrt(squares / model_width + EPSILON)[:, None] * ln1_gain).astype(
        jnp.bfloat16
    )
    q_sum, key_sum, v_sum, gate = lax.psum(
        (
            jnp.dot(normed1, wq, preferred_element_type=jnp.float32),
            jnp.dot(normed1, wk, preferred_element_type=jnp.float32),
            jnp.dot(normed1, wv, preferred_element_type=jnp.float32),
            jnp.dot(normed1, wg, preferred_element_type=jnp.float32),
        ),
        "seq",
    )
    query_rows_all = apply_rotary(
        head_norm(q_sum.reshape(token_count, query_heads, head_dim), q_gain), token_position
    ) * head_dim ** (-0.5)
    query_rows_all = query_rows_all.astype(jnp.bfloat16).reshape(
        requests, tree_size, kv_heads, query_group_size, head_dim
    )
    draft_keys = apply_rotary(
        head_norm(key_sum.reshape(token_count, kv_heads, head_dim), key_gain), token_position
    ).astype(jnp.bfloat16)
    draft_values = v_sum.astype(jnp.bfloat16)
    tree_keys = draft_keys.reshape(requests, tree_size, kv_heads, head_dim)
    tree_values = draft_values.reshape(requests, tree_size, kv_heads, head_dim)
    cache_keys = key_cache.reshape(requests, slot_count, kv_heads, head_dim)
    cache_values = value_cache.reshape(requests, slot_count, kv_heads, head_dim)
    slot_ids = slot_start + jnp.arange(slot_count, dtype=jnp.int32)
    local_state = cache_part(
        query_rows_all, cache_keys, cache_values, slot_ids[None, :] < lengths[:, None]
    )
    local_peak, local_mass, local_sum = local_state
    cache_peak = lax.pmax(local_peak, "seq")
    factor = jnp.exp(local_peak - cache_peak)
    cache_mass, cache_sum = lax.psum((local_mass * factor, local_sum * factor[..., None]), "seq")
    tree_scores = jnp.einsum(
        "rikgd,rjkd->rkgij", query_rows_all, tree_keys, preferred_element_type=jnp.float32
    )
    valid_node = (parent_links > 0.5)[:, None, None, :, :]
    row_top = jnp.maximum(
        cache_peak, jnp.max(jnp.where(valid_node, tree_scores, NEGATIVE), axis=-1)
    )
    tree_weights = jnp.where(valid_node, jnp.exp(tree_scores - row_top[..., None]), 0.0)
    cache_factor = jnp.exp(cache_peak - row_top)
    row_mass = cache_mass * cache_factor + jnp.sum(tree_weights, axis=-1)
    weighted = cache_sum * cache_factor[..., None] + jnp.einsum(
        "rkgij,rjkd->rkgid",
        tree_weights.astype(jnp.bfloat16),
        tree_values,
        preferred_element_type=jnp.float32,
    )
    attention_result = jnp.transpose(weighted / row_mass[..., None], (0, 3, 1, 2, 4)).reshape(
        token_count, query_heads * head_dim
    )
    gated = (attention_result * jax.nn.sigmoid(gate)).astype(jnp.bfloat16)
    attn_sum = lax.psum(jnp.dot(gated, wo, preferred_element_type=jnp.float32), "tp")
    middle = (hidden_wide + attn_sum).astype(jnp.bfloat16)
    middle_wide = middle.astype(jnp.float32)
    squares_mid = lax.psum(jnp.sum(middle_wide * middle_wide, axis=1), "seq")
    normed2 = (
        middle_wide * lax.rsqrt(squares_mid / model_width + EPSILON)[:, None] * ln2_gain
    ).astype(jnp.bfloat16)
    gate_part, up_part = lax.psum(
        (
            jnp.dot(normed2, w_gate, preferred_element_type=jnp.float32),
            jnp.dot(normed2, w_up, preferred_element_type=jnp.float32),
        ),
        "seq",
    )
    activated = (jax.nn.silu(gate_part) * up_part).astype(jnp.bfloat16)
    down_part = jnp.dot(activated, w_down, preferred_element_type=jnp.float32)
    down_sum = lax.psum(down_part, "tp")
    next_hidden = (middle_wide + down_sum).astype(jnp.bfloat16)
    next_wide = next_hidden.astype(jnp.float32)
    squares_last = lax.psum(jnp.sum(next_wide * next_wide, axis=1), "seq")
    normed3 = (
        next_wide * lax.rsqrt(squares_last / model_width + EPSILON)[:, None] * last_gain
    ).astype(jnp.bfloat16)
    logits = jnp.dot(
        lax.all_gather(normed3, "seq", axis=1, tiled=True),
        head_weight,
        preferred_element_type=jnp.float32,
    )
    logits = logits * jnp.repeat(inv_temp, tree_size)[:, None]
    vocab_top = lax.pmax(jnp.max(logits, axis=1), ("seq", "tp"))
    vocab_total = lax.psum(jnp.sum(jnp.exp(logits - vocab_top[:, None]), axis=1), ("seq", "tp"))
    logprobs = logits - (vocab_top + jnp.log(vocab_total))[:, None]
    accepted_rows = parent_links[jnp.arange(requests), accepted]
    target = token_position.reshape(requests, tree_size)
    slot_all = slot_start + jnp.arange(slot_count, dtype=jnp.int32)
    placed = (slot_all[None, :, None] == target[:, None, :]).astype(jnp.float32) * accepted_rows[
        :, None, :
    ]
    hits = (jnp.sum(placed, axis=2) > 0.5)[:, :, None]
    placed_low = placed.astype(jnp.bfloat16)
    moved_keys = jnp.einsum(
        "rca,rae->rce",
        placed_low,
        draft_keys.reshape(requests, tree_size, kv_heads * head_dim),
        preferred_element_type=jnp.float32,
    ).astype(jnp.bfloat16)
    moved_values = jnp.einsum(
        "rca,rae->rce",
        placed_low,
        draft_values.reshape(requests, tree_size, kv_heads * head_dim),
        preferred_element_type=jnp.float32,
    ).astype(jnp.bfloat16)
    updated_key_cache = jnp.where(hits, moved_keys, key_cache)
    updated_value_cache = jnp.where(hits, moved_values, value_cache)
    return (logprobs, next_hidden, updated_key_cache, updated_value_cache)


def solution(mesh):
    in_specs = (
        P(None, "seq"),
        P("seq"),
        P("seq", "tp"),
        P("seq", "tp"),
        P("seq", "tp"),
        P("seq", "tp"),
        P(),
        P(),
        P("tp", "seq"),
        P("seq"),
        P("seq", "tp"),
        P("seq", "tp"),
        P("tp", "seq"),
        P("seq"),
        P(None, ("seq", "tp")),
        P(),
        P(None, "seq", "tp"),
        P(None, "seq", "tp"),
        P(),
        P(),
        P(),
    )
    out_specs = (P(None, ("seq", "tp")), P(None, "seq"), P(None, "seq", "tp"), P(None, "seq", "tp"))
    return jax.shard_map(
        on_device, mesh=mesh, in_specs=in_specs, out_specs=out_specs, check_vma=False
    )
```

profile of v0, /device:TPU:1, one launch (start us, length us, event | category | flops | bytes accessed | tf_op | source)
XLA Modules:
  0.0 1792.0 jit_solution(4256023891018787633)
XLA Ops:
  7.2 0.8 fusion.51
  8.1 122.9 %psum.98 = f32[384]{0:T(512)S(1)} all-reduce(f32[384]{0:T(512)S(1)} %fusion.51), channel_id=1, replica_groups=mesh['seq'=64,'tp'=8] {'seq'}, use_global_device_ids=true, to_apply=%region_1.0 | all-reduce | flops 384 | bytes 3072 | tf_op jit(solution)/shard_map/psum | solution.py:95
  130.9 1.8 fusion.88
  132.8 1.4 convolution_minimum_fusion.5
  134.3 0.3 convolution_minimum_fusion.4
  134.7 0.3 convolution_minimum_fusion.3
  135.0 0.3 convolution_minimum_fusion.2
  135.3 0.3 convolution_minimum_fusion.1
  135.6 0.3 fusion.59
  136.2 1.0 fusion.86
  137.2 0.4 multiply_cosine_fusion.1
  137.7 1.1 fusion.82
  138.7 269.0 %all-reduce.8.cloned.1.call-done = f32[384,2,128]{0,2,1:T(8,128)} async-done(((f32[384,2,128]{0,2,1:T(8,128)}), f32[384,2,128]{0,2,1:T(8,128)}) %all-reduce.8.cloned.1.call-update) | async-done | bytes 393232 | tf_op jit(solution)/shard_map/psum | solution.py:99
  407.7 1.0 multiply_reduce_fusion
  408.8 1.1 multiply_multiply_fusion
  410.2 0.2 copy.31
  411.0 0.4 copy-done.2
  411.4 0.4 select_reduce_fusion
  411.8 114.2 %pmax.14 = f32[8,1,2,48]{3,2,0,1:T(2,128)S(1)} all-reduce(f32[8,1,2,48]{3,2,0,1:T(2,128)S(1)} %bitcast.134), channel_id=1, replica_groups=mesh['seq'=64,'tp'=8] {'seq'}, use_global_device_ids=true, to_apply=%region_6.0 | all-reduce | flops 768 | bytes 6144 | tf_op jit(solution)/shard_map/pmax | solution.py:127
  526.1 0.4 fusion.6
  526.5 1.1 fusion.2
  527.6 0.3 fusion.84
  528.0 219.4 %all-reduce.13 = (bf16[384,128]{1,0:T(8,128)(2,1)S(1)}, f32[8,1,2,48]{3,2,0,1:T(2,128)S(1)}) all-reduce(f32[384,128]{1,0:T(8,128)S(1)} %fusion.84, f32[8,1,2,48]{3,2,0,1:T(2,128)S(1)} %get-tuple-element.32), channel_id=1, replica_groups=mesh['seq'=64,'tp'=8] {'seq'}, use_global_device_ids=true, to_apply=%region_11.12 | all-reduce | flops 49920 | bytes 301056 | tf_op jit(solution)/shard_map/psum | solution.py:99
  747.3 74.5 %all-reduce.12.cloned.1.call-done = (f32[8,1,2,48,128]{4,3,2,0,1:T(8,128)}, f32[384,128]{1,0:T(8,128)}, f32[384,256]{1,0:T(8,128)}) async-done(((f32[8,1,2,48,128]{4,3,2,0,1:T(8,128)}, f32[384,128]{1,0:T(8,128)}, f32[384,256]{1,0:T(8,128)}), (f32[8,1,2,48,128]{4,3,2,0,1:T(8,128)}, f32[384,128]{1,0:T(8,128)}, f32[384,256]{1,0:T(8,128)})) %all-reduce.12.cloned.1.call-update) | async-done | bytes 983056 | tf_op jit(solution)/shard_map/psum | solution.py:129
  821.8 1.1 multiply_reduce_fusion.1
  822.9 1.1 multiply_bitcast_fusion
  824.0 0.8 fusion.25
  824.9 0.4 select_reduce_fusion.2
  825.4 0.4 fusion.5
  826.1 0.4 copy-done.17
  826.4 0.2 fusion.43
  826.7 39.8 %psum.105 = f32[384,32]{0,1:T(8,128)S(1)} all-reduce(f32[384,32]{0,1:T(8,128)S(1)} %fusion.43), channel_id=1, replica_groups=mesh['seq'=64,'tp'=8] {'tp'}, use_global_device_ids=true, to_apply=%region_16.17 | all-reduce | flops 12288 | bytes 98304 | tf_op jit(solution)/shard_map/psum | solution.py:150
  866.5 110.1 %psum.106 = f32[384]{0:T(512)S(1)} all-reduce(f32[384]{0:T(512)S(1)} %get-tuple-element.21), channel_id=1, replica_groups=mesh['seq'=64,'tp'=8] {'seq'}, use_global_device_ids=true, to_apply=%region_18.19 | all-reduce | flops 384 | bytes 3072 | tf_op jit(solution)/shard_map/psum | solution.py:153
  976.7 1.4 fusion.63
  978.1 1.4 fusion.65
  979.6 295.4 %all-reduce.10.cloned.1.call-done = (f32[384,768]{1,0:T(8,128)}, f32[384,768]{1,0:T(8,128)}) async-done(((f32[384,768]{1,0:T(8,128)}, f32[384,768]{1,0:T(8,128)}), (f32[384,768]{1,0:T(8,128)}, f32[384,768]{1,0:T(8,128)})) %all-reduce.10.cloned.1.call-update) | async-done | bytes 2359312 | tf_op jit(solution)/shard_map/psum | solution.py:157
  1275.1 2.1 fusion.8
  1277.2 30.1 %psum.109 = f32[384,32]{0,1:T(8,128)S(1)} all-reduce(f32[384,32]{0,1:T(8,128)S(1)} %fusion.8), channel_id=1, replica_groups=mesh['seq'=64,'tp'=8] {'tp'}, use_global_device_ids=true, to_apply=%region_21.22 | all-reduce | flops 12288 | bytes 98304 | tf_op jit(solution)/shard_map/psum | solution.py:166
  1307.3 112.8 %psum.110 = f32[384]{0:T(512)S(1)} all-reduce(f32[384]{0:T(512)S(1)} %get-tuple-element.19), channel_id=1, replica_groups=mesh['seq'=64,'tp'=8] {'seq'}, use_global_device_ids=true, to_apply=%region_23.24 | all-reduce | flops 384 | bytes 3072 | tf_op jit(solution)/shard_map/psum | solution.py:169
  1420.1 0.7 fusion.50
  1421.1 0.6 gather_fusion
  1421.9 1.7 fusion.1
  1423.5 1.6 fusion
  1425.1 148.8 %all-gather.2.cloned.1.call-done = bf16[384,2048]{0,1:T(8,128)(2,1)} async-done(((bf16[384,32]{0,1:T(8,128)(2,1)}), bf16[384,2048]{0,1:T(8,128)(2,1)}) %all-gather.2.cloned.1.call-update) | async-done | bytes 1572880 | tf_op jit(solution)/shard_map/all_gather | solution.py:174
  1573.9 2.2 fusion.93
  1576.1 109.6 %pmax.15 = f32[384]{0:T(512)S(1)} all-reduce(f32[384]{0:T(512)S(1)} %get-tuple-element.41), channel_id=1, replica_groups=mesh['seq'=64,'tp'=8] {'seq','tp'}, use_global_device_ids=true, to_apply=%region_25.26 | all-reduce | flops 384 | bytes 3072 | tf_op jit(solution)/shard_map/pmax | solution.py:179
  1685.8 98.8 %psum.111 = f32[384]{0:T(512)S(1)} all-reduce(f32[384]{0:T(512)S(1)} %exponential_reduce_fusion), channel_id=1, replica_groups=mesh['seq'=64,'tp'=8] {'seq','tp'}, use_global_device_ids=true, to_apply=%region_27.28 | all-reduce | flops 384 | bytes 3072 | tf_op jit(solution)/shard_map/psum | solution.py:180
  1784.6 0.9 copy.35
  (84 shorter events, 2.6 us)
Async XLA Ops:
  7.2 1566.7 %copy-start = (bf16[2048,256]{1,0:T(8,128)(2,1)S(1)}, bf16[2048,256]{1,0:T(8,128)(2,1)}, u32[]{:S(2)}) copy-start(bf16[2048,256]{1,0:T(8,128)(2,1)} %param.35) | copy-start | bytes 3145732
  7.2 400.6 %all-reduce.8.cloned.1.call-start = ((), (), s32[]{:S(2)}) async-start(), calls=%async_computation | async-start | bytes 786432 | tf_op jit(solution)/shard_map/psum | solution.py:99
  132.7 689.1 %all-reduce.12.cloned.1.call-start = ((), (), s32[]{:S(2)}) async-start(), calls=%async_computation.3 | async-start | bytes 1966080 | tf_op jit(solution)/shard_map/psum | solution.py:129
  134.6 1.4 copy-start.12
  134.6 1.6 copy-start.1
  134.6 1.6 copy-start.8
  134.6 1.6 copy-start.9
  135.0 2.7 copy-start.7
  135.3 273.5 %copy-start.16 = (f32[128]{0:T(128)S(1)}, f32[128]{0:T(128)}, u32[]{:S(2)}) copy-start(f32[128]{0:T(128)} %param.27) | copy-start | bytes 1540
  410.4 1.0 copy-start.2
  411.4 115.0 %copy-start.3 = (bf16[8,256,128]{2,1,0:T(8,128)(2,1)S(1)}, bf16[8,256,128]{2,1,0:T(8,128)(2,1)}, u32[]{:S(2)}) copy-start(bf16[8,256,128]{2,1,0:T(8,128)(2,1)} %param.38) | copy-start | bytes 1572868
  526.5 1.2 copy-start.10
  527.6 295.3 %copy-start.13 = (f32[128]{0:T(128)S(1)}, f32[128]{0:T(128)}, u32[]{:S(2)}) copy-start(f32[128]{0:T(128)} %param.28) | copy-start | bytes 1540
  527.6 747.5 %all-reduce.10.cloned.1.call-start = ((), (), s32[]{:S(2)}) async-start(), calls=%async_computation.2 | async-start | bytes 4718592 | tf_op jit(solution)/shard_map/psum | solution.py:157
  822.9 2.5 copy-start.18
  825.4 1.0 copy-start.17
  825.4 1.0 copy-start.20
  826.0 150.7 %copy-start.5 = (bf16[32,768]{1,0:T(8,128)(2,1)S(1)}, bf16[32,768]{1,0:T(8,128)(2,1)}, u32[]{:S(2)}) copy-start(bf16[32,768]{1,0:T(8,128)(2,1)} %param.32) | copy-start | bytes 147460
  826.0 150.7 %copy-start.11 = (f32[32]{0:T(128)S(1)}, f32[32]{0:T(128)}, u32[]{:S(2)}) copy-start(f32[32]{0:T(128)} %param.30) | copy-start | bytes 388
  826.7 151.5 %copy-start.6 = (bf16[32,768]{1,0:T(8,128)(2,1)S(1)}, bf16[32,768]{1,0:T(8,128)(2,1)}, u32[]{:S(2)}) copy-start(bf16[32,768]{1,0:T(8,128)(2,1)} %param.31) | copy-start | bytes 147460
  979.5 295.5 %copy-start.19 = (bf16[768,32]{0,1:T(8,128)(2,1)S(1)}, bf16[768,32]{0,1:T(8,128)(2,1)}, u32[]{:S(2)}) copy-start(bf16[768,32]{0,1:T(8,128)(2,1)} %param.33) | copy-start | bytes 147460
  979.6 594.3 %all-gather.2.cloned.1.call-start = ((), (), s32[]{:S(2)}) async-start(), calls=%async_computation.1 | async-start | bytes 1597440 | tf_op jit(solution)/shard_map/all_gather | solution.py:174
  1275.0 145.0 %copy-start.14 = (f32[32]{0:T(128)S(1)}, f32[32]{0:T(128)}, u32[]{:S(2)}) copy-start(f32[32]{0:T(128)} %param.34) | copy-start | bytes 388
  1275.0 145.7 %copy-start.15 = (f32[8]{0:T(128)S(1)}, f32[8]{0:T(128)}, u32[]{:S(2)}) copy-start(f32[8]{0:T(128)} %param.36) | copy-start | bytes 100
  1275.0 146.0 %copy-start.21 = (s32[8]{0:T(128)S(1)}, s32[8]{0:T(128)}, u32[]{:S(2)}) copy-start(s32[8]{0:T(128)} %param.41) | copy-start | bytes 100
  1307.3 117.8 %copy-start.4 = (bf16[384,32]{0,1:T(8,128)(2,1)}, bf16[384,32]{0,1:T(8,128)(2,1)S(1)}, u32[]{:S(2)}) copy-start(bf16[384,32]{0,1:T(8,128)(2,1)S(1)} %get-tuple-element.20) | copy-start | bytes 73732
Sparse Core Ops, SparseCore 0:
  132.9 274.8 all-reduce.7
  527.7 294.0 all-reduce.11
  979.7 295.2 all-reduce.9
  1420.9 152.9 all-gather.1
where the time goes:
time: 1790 us
  blocking collectives  958 us (54%)
  waiting for transfers between devices  788 us (44%)
  matrix products  19.9 us (1%)
    psum x1, waiting for transfers between devices, on_device(): lax.psum((jnp.dot(normed2, w_gate, preferred_element_type=jnp.float32), j...  295 us
    psum x1, waiting for transfers between devices, on_device(): lax.psum((jnp.dot(normed1, wq, preferred_element_type=jnp.float32), jnp.d...  269 us
    psum x1, blocking collectives, on_device(): lax.psum((jnp.dot(normed1, wq, preferred_element_type=jnp.float32), jnp.d...  219 us
    all_gather x1, waiting for transfers between devices, on_device(): lax.all_gather(normed3, 'seq', axis=1, tiled=True)  149 us
    psum x1, blocking collectives, on_device(): squares = lax.psum(jnp.sum(hidden_wide * hidden_wide, axis=1), 'seq')  123 us
    pmax x1, blocking collectives, on_device(): cache_peak = lax.pmax(local_peak, 'seq')  114 us
    psum x1, blocking collectives, on_device(): squares_last = lax.psum(jnp.sum(next_wide * next_wide, axis=1), 'seq')  113 us
    psum x1, blocking collectives, on_device(): squares_mid = lax.psum(jnp.sum(middle_wide * middle_wide, axis=1), 'seq')  110 us
  transfers between devices with their start and end apart: 4, of which 4 were waited for; matrix products, arithmetic and copies ran while one was open for 1% of the time, Pallas kernels for 0%

commit v1 on v0

--- a/solution.py
+++ b/solution.py
@@ -177,7 +177,9 @@
     )
     logits = logits * jnp.repeat(inv_temp, tree_size)[:, None]
     vocab_top = lax.pmax(jnp.max(logits, axis=1), ("seq", "tp"))
-    vocab_total = lax.psum(jnp.sum(jnp.exp(logits - vocab_top[:, None]), axis=1), ("seq", "tp"))
+    vocab_total = jnp.sum(jnp.exp(logits - vocab_top[:, None]), axis=1)
+    for k in ("tp", "seq"):
+        vocab_total = lax.psum(vocab_total, axis_name=k)
     logprobs = logits - (vocab_top + jnp.log(vocab_total))[:, None]
     accepted_rows = parent_links[jnp.arange(requests), accepted]
     target = token_position.reshape(requests, tree_size)

time: 1790 us -> 1850 us (1.034); the launches traced: 1790 us -> 1820 us
  blocking collectives: 958 us -> 984 us
    psum x1 -> x2, blocking collectives: 98.8 us -> 125 us  [on_device(): vocab_total = lax.psum(vocab_total, axis_name=k)]
where the time goes in v1:
time: 1850 us; the launch traced here: 1820 us
  blocking collectives  984 us (53%)
  waiting for transfers between devices  788 us (43%)
  matrix products  19.9 us (1%)
    psum x1, waiting for transfers between devices, on_device(): lax.psum((jnp.dot(normed2, w_gate, preferred_element_type=jnp.float32), j...  295 us
    psum x1, waiting for transfers between devices, on_device(): lax.psum((jnp.dot(normed1, wq, preferred_element_type=jnp.float32), jnp.d...  269 us
    psum x1, blocking collectives, on_device(): lax.psum((jnp.dot(normed1, wq, preferred_element_type=jnp.float32), jnp.d...  219 us
    all_gather x1, waiting for transfers between devices, on_device(): lax.all_gather(normed3, 'seq', axis=1, tiled=True)  149 us
    psum x2, blocking collectives, on_device(): vocab_total = lax.psum(vocab_total, axis_name=k)  125 us
    psum x1, blocking collectives, on_device(): squares = lax.psum(jnp.sum(hidden_wide * hidden_wide, axis=1), 'seq')  123 us
    pmax x1, blocking collectives, on_device(): cache_peak = lax.pmax(local_peak, 'seq')  114 us
    psum x1, blocking collectives, on_device(): squares_last = lax.psum(jnp.sum(next_wide * next_wide, axis=1), 'seq')  113 us
  transfers between devices with their start and end apart: 4, of which 4 were waited for; matrix products, arithmetic and copies ran while one was open for 1% of the time, Pallas kernels for 0%

profile of v1, /device:TPU:1, one launch (start us, length us, event | category | flops | bytes accessed | tf_op | source)
XLA Modules:
  0.0 1818.2 jit_solution(14181584428916280802)
XLA Ops:
  7.2 0.8 fusion.51
  8.1 122.9 %psum.105 = f32[384]{0:T(512)S(1)} all-reduce(f32[384]{0:T(512)S(1)} %fusion.51), channel_id=1, replica_groups=mesh['seq'=64,'tp'=8] {'seq'}, use_global_device_ids=true, to_apply=%region_1.0 | all-reduce | flops 384 | bytes 3072 | tf_op jit(solution)/shard_map/psum | solution.py:95
  130.9 1.8 fusion.88
  132.8 1.4 convolution_minimum_fusion.5
  134.3 0.3 convolution_minimum_fusion.4
  134.7 0.3 convolution_minimum_fusion.3
  135.0 0.3 convolution_minimum_fusion.2
  135.3 0.3 convolution_minimum_fusion.1
  135.6 0.3 fusion.59
  136.2 1.0 fusion.86
  137.2 0.4 multiply_cosine_fusion.1
  137.7 1.1 fusion.82
  138.7 269.0 %all-reduce.8.cloned.1.call-done = f32[384,2,128]{0,2,1:T(8,128)} async-done(((f32[384,2,128]{0,2,1:T(8,128)}), f32[384,2,128]{0,2,1:T(8,128)}) %all-reduce.8.cloned.1.call-update) | async-done | bytes 393232 | tf_op jit(solution)/shard_map/psum | solution.py:99
  407.7 1.0 multiply_reduce_fusion
  408.8 1.1 multiply_multiply_fusion
  411.0 0.4 copy-done.2
  411.4 0.4 select_reduce_fusion
  411.8 114.2 %pmax.14 = f32[8,1,2,48]{3,2,0,1:T(2,128)S(1)} all-reduce(f32[8,1,2,48]{3,2,0,1:T(2,128)S(1)} %bitcast.134), channel_id=1, replica_groups=mesh['seq'=64,'tp'=8] {'seq'}, use_global_device_ids=true, to_apply=%region_6.0 | all-reduce | flops 768 | bytes 6144 | tf_op jit(solution)/shard_map/pmax | solution.py:127
  526.1 0.4 fusion.6
  526.5 1.1 fusion.2
  527.6 0.3 fusion.84
  528.0 219.4 %all-reduce.13 = (bf16[384,128]{1,0:T(8,128)(2,1)S(1)}, f32[8,1,2,48]{3,2,0,1:T(2,128)S(1)}) all-reduce(f32[384,128]{1,0:T(8,128)S(1)} %fusion.84, f32[8,1,2,48]{3,2,0,1:T(2,128)S(1)} %get-tuple-element.32), channel_id=1, replica_groups=mesh['seq'=64,'tp'=8] {'seq'}, use_global_device_ids=true, to_apply=%region_11.12 | all-reduce | flops 49920 | bytes 301056 | tf_op jit(solution)/shard_map/psum | solution.py:99
  747.3 74.5 %all-reduce.12.cloned.1.call-done = (f32[8,1,2,48,128]{4,3,2,0,1:T(8,128)}, f32[384,128]{1,0:T(8,128)}, f32[384,256]{1,0:T(8,128)}) async-done(((f32[8,1,2,48,128]{4,3,2,0,1:T(8,128)}, f32[384,128]{1,0:T(8,128)}, f32[384,256]{1,0:T(8,128)}), (f32[8,1,2,48,128]{4,3,2,0,1:T(8,128)}, f32[384,128]{1,0:T(8,128)}, f32[384,256]{1,0:T(8,128)})) %all-reduce.12.cloned.1.call-update) | async-done | bytes 983056 | tf_op jit(solution)/shard_map/psum | solution.py:129
  821.8 1.1 multiply_reduce_fusion.1
  822.9 1.1 multiply_bitcast_fusion
  824.0 0.8 fusion.25
  824.9 0.4 select_reduce_fusion.2
  825.4 0.4 fusion.5
  826.1 0.4 copy-done.17
  826.4 0.2 fusion.43
  826.7 39.8 %psum.112 = f32[384,32]{0,1:T(8,128)S(1)} all-reduce(f32[384,32]{0,1:T(8,128)S(1)} %fusion.43), channel_id=1, replica_groups=mesh['seq'=64,'tp'=8] {'tp'}, use_global_device_ids=true, to_apply=%region_16.17 | all-reduce | flops 12288 | bytes 98304 | tf_op jit(solution)/shard_map/psum | solution.py:150
  866.5 110.1 %psum.113 = f32[384]{0:T(512)S(1)} all-reduce(f32[384]{0:T(512)S(1)} %get-tuple-element.21), channel_id=1, replica_groups=mesh['seq'=64,'tp'=8] {'seq'}, use_global_device_ids=true, to_apply=%region_18.19 | all-reduce | flops 384 | bytes 3072 | tf_op jit(solution)/shard_map/psum | solution.py:153
  976.7 1.4 fusion.63
  978.1 1.4 fusion.65
  979.6 295.4 %all-reduce.10.cloned.1.call-done = (f32[384,768]{1,0:T(8,128)}, f32[384,768]{1,0:T(8,128)}) async-done(((f32[384,768]{1,0:T(8,128)}, f32[384,768]{1,0:T(8,128)}), (f32[384,768]{1,0:T(8,128)}, f32[384,768]{1,0:T(8,128)})) %all-reduce.10.cloned.1.call-update) | async-done | bytes 2359312 | tf_op jit(solution)/shard_map/psum | solution.py:157
  1275.1 2.1 fusion.8
  1277.2 30.1 %psum.116 = f32[384,32]{0,1:T(8,128)S(1)} all-reduce(f32[384,32]{0,1:T(8,128)S(1)} %fusion.8), channel_id=1, replica_groups=mesh['seq'=64,'tp'=8] {'tp'}, use_global_device_ids=true, to_apply=%region_21.22 | all-reduce | flops 12288 | bytes 98304 | tf_op jit(solution)/shard_map/psum | solution.py:166
  1307.3 112.8 %psum.117 = f32[384]{0:T(512)S(1)} all-reduce(f32[384]{0:T(512)S(1)} %get-tuple-element.19), channel_id=1, replica_groups=mesh['seq'=64,'tp'=8] {'seq'}, use_global_device_ids=true, to_apply=%region_23.24 | all-reduce | flops 384 | bytes 3072 | tf_op jit(solution)/shard_map/psum | solution.py:169
  1420.1 0.7 fusion.50
  1421.1 0.6 gather_fusion
  1421.9 1.7 fusion.1
  1423.5 1.6 fusion
  1425.1 148.8 %all-gather.2.cloned.1.call-done = bf16[384,2048]{0,1:T(8,128)(2,1)} async-done(((bf16[384,32]{0,1:T(8,128)(2,1)}), bf16[384,2048]{0,1:T(8,128)(2,1)}) %all-gather.2.cloned.1.call-update) | async-done | bytes 1572880 | tf_op jit(solution)/shard_map/all_gather | solution.py:174
  1573.9 2.2 fusion.93
  1576.1 109.6 %pmax.15 = f32[384]{0:T(512)S(1)} all-reduce(f32[384]{0:T(512)S(1)} %get-tuple-element.41), channel_id=1, replica_groups=mesh['seq'=64,'tp'=8] {'seq','tp'}, use_global_device_ids=true, to_apply=%region_25.26 | all-reduce | flops 384 | bytes 3072 | tf_op jit(solution)/shard_map/pmax | solution.py:179
  1685.8 12.4 psum.118
  1698.2 112.5 %psum.119 = f32[384]{0:T(512)S(1)} all-reduce(f32[384]{0:T(512)S(1)} %psum.118), channel_id=1, replica_groups=mesh['seq'=64,'tp'=8] {'seq'}, use_global_device_ids=true, to_apply=%region_28.29 | all-reduce | flops 384 | bytes 3072 | tf_op jit(solution)/shard_map/psum | solution.py:182
  1810.7 0.9 copy.35
  (85 shorter events, 2.8 us)
Async XLA Ops:
  7.2 1566.7 %copy-start = (bf16[2048,256]{1,0:T(8,128)(2,1)S(1)}, bf16[2048,256]{1,0:T(8,128)(2,1)}, u32[]{:S(2)}) copy-start(bf16[2048,256]{1,0:T(8,128)(2,1)} %param.35) | copy-start | bytes 3145732
  7.2 400.6 %all-reduce.8.cloned.1.call-start = ((), (), s32[]{:S(2)}) async-start(), calls=%async_computation | async-start | bytes 786432 | tf_op jit(solution)/shard_map/psum | solution.py:99
  132.7 689.1 %all-reduce.12.cloned.1.call-start = ((), (), s32[]{:S(2)}) async-start(), calls=%async_computation.3 | async-start | bytes 1966080 | tf_op jit(solution)/shard_map/psum | solution.py:129
  134.6 1.4 copy-start.12
  134.6 1.6 copy-start.1
  134.6 1.6 copy-start.8
  134.6 1.6 copy-start.9
  135.0 2.7 copy-start.7
  135.3 273.5 %copy-start.16 = (f32[128]{0:T(128)S(1)}, f32[128]{0:T(128)}, u32[]{:S(2)}) copy-start(f32[128]{0:T(128)} %param.27) | copy-start | bytes 1540
  410.4 1.0 copy-start.2
  411.4 115.0 %copy-start.3 = (bf16[8,256,128]{2,1,0:T(8,128)(2,1)S(1)}, bf16[8,256,128]{2,1,0:T(8,128)(2,1)}, u32[]{:S(2)}) copy-start(bf16[8,256,128]{2,1,0:T(8,128)(2,1)} %param.38) | copy-start | bytes 1572868
  526.5 1.2 copy-start.10
  527.6 295.3 %copy-start.13 = (f32[128]{0:T(128)S(1)}, f32[128]{0:T(128)}, u32[]{:S(2)}) copy-start(f32[128]{0:T(128)} %param.28) | copy-start | bytes 1540
  527.6 747.5 %all-reduce.10.cloned.1.call-start = ((), (), s32[]{:S(2)}) async-start(), calls=%async_computation.2 | async-start | bytes 4718592 | tf_op jit(solution)/shard_map/psum | solution.py:157
  822.9 2.5 copy-start.18
  825.4 1.0 copy-start.17
  825.4 1.0 copy-start.20
  826.0 150.7 %copy-start.5 = (bf16[32,768]{1,0:T(8,128)(2,1)S(1)}, bf16[32,768]{1,0:T(8,128)(2,1)}, u32[]{:S(2)}) copy-start(bf16[32,768]{1,0:T(8,128)(2,1)} %param.32) | copy-start | bytes 147460
  826.0 150.7 %copy-start.11 = (f32[32]{0:T(128)S(1)}, f32[32]{0:T(128)}, u32[]{:S(2)}) copy-start(f32[32]{0:T(128)} %param.30) | copy-start | bytes 388
  826.7 151.5 %copy-start.6 = (bf16[32,768]{1,0:T(8,128)(2,1)S(1)}, bf16[32,768]{1,0:T(8,128)(2,1)}, u32[]{:S(2)}) copy-start(bf16[32,768]{1,0:T(8,128)(2,1)} %param.31) | copy-start | bytes 147460
  979.5 295.5 %copy-start.19 = (bf16[768,32]{0,1:T(8,128)(2,1)S(1)}, bf16[768,32]{0,1:T(8,128)(2,1)}, u32[]{:S(2)}) copy-start(bf16[768,32]{0,1:T(8,128)(2,1)} %param.33) | copy-start | bytes 147460
  979.6 594.3 %all-gather.2.cloned.1.call-start = ((), (), s32[]{:S(2)}) async-start(), calls=%async_computation.1 | async-start | bytes 1597440 | tf_op jit(solution)/shard_map/all_gather | solution.py:174
  1275.0 145.0 %copy-start.14 = (f32[32]{0:T(128)S(1)}, f32[32]{0:T(128)}, u32[]{:S(2)}) copy-start(f32[32]{0:T(128)} %param.34) | copy-start | bytes 388
  1275.0 145.7 %copy-start.15 = (f32[8]{0:T(128)S(1)}, f32[8]{0:T(128)}, u32[]{:S(2)}) copy-start(f32[8]{0:T(128)} %param.36) | copy-start | bytes 100
  1275.0 146.0 %copy-start.21 = (s32[8]{0:T(128)S(1)}, s32[8]{0:T(128)}, u32[]{:S(2)}) copy-start(s32[8]{0:T(128)} %param.41) | copy-start | bytes 100
  1307.3 117.8 %copy-start.4 = (bf16[384,32]{0,1:T(8,128)(2,1)}, bf16[384,32]{0,1:T(8,128)(2,1)S(1)}, u32[]{:S(2)}) copy-start(bf16[384,32]{0,1:T(8,128)(2,1)S(1)} %get-tuple-element.20) | copy-start | bytes 73732
Sparse Core Ops, SparseCore 0:
  132.9 274.8 all-reduce.7
  527.7 294.0 all-reduce.11
  979.7 295.2 all-reduce.9
  1420.9 152.9 all-gather.1
